TPU v7x, 32 devices: a whole 2x2x4 slice. The times are simulated.
32 devices in a mesh: band: 4 (over z), grid: 8 (over y, x, core).
Axes of the slice: x: 2, y: 2, z: 4, core: 2. Of those that a mesh axis runs over, the one named last changes fastest.
Arguments:
- orbitals: bfloat16 [8, 256, 256, 256], P('band', 'grid'), may hold values from -60 to 60
- potential: float32 [256, 256, 256], P('grid'), may hold values from -2 to 1
Outputs:
- rotated: bfloat16 [8, 256, 256, 256], P('band', 'grid')
- projected: float32 [8, 8], replicated
All inputs are finite; a program needn't handle non-finite values. Where the computation divides by a largest or mean magnitude, that divisor is 1e-20 or more.
Results may differ from a plain program's by a relative error of at most 0.0005.
The roundings to bfloat16 on the way count: a program that leaves them out, or rounds other values in their place, can miss the bound.
Values may be sent and summed in bfloat16 or wider, within the bound.
A program may use at most 192 MiB of HBM per device.

v0:
```python
import math
import jax
import jax.numpy as jnp
from jax import lax
from jax.sharding import PartitionSpec as P

NS_ITERS = 6
CENTER = 9.5
HALF_WIDTH = 6.5


def second_derivative(length):
    index = jnp.arange(length, dtype=jnp.int32)
    product = index[:, None] * index[None, :] % length
    angles = product.astype(jnp.float32) * (2.0 * math.pi / length)
    freq = jnp.minimum(index, length - index).astype(jnp.float32)
    weight = -((2.0 * math.pi / length * freq) ** 2) / length
    cosines = jnp.cos(angles)
    sines = jnp.sin(angles)
    matrix = jnp.dot(cosines * weight[None, :], cosines.T, precision=lax.Precision.HIGHEST)
    matrix = matrix + jnp.dot(sines * weight[None, :], sines.T, precision=lax.Precision.HIGHEST)
    return matrix.astype(jnp.bfloat16)


def apply_ham(field, potential, k_x, k_y, k_z):
    depth = field.shape[3]
    term_z = jnp.dot(field.reshape(-1, depth), k_z, preferred_element_type=jnp.float32).reshape(
        field.shape
    )
    term_y = jnp.einsum("oxjz,jy->oxyz", field, k_y, preferred_element_type=jnp.float32)
    derived = jnp.einsum(
        "ojyz,jx->oxyz",
        lax.all_to_all(field, "grid", split_axis=2, concat_axis=1, tiled=True),
        k_x,
        preferred_element_type=jnp.float32,
    ).astype(jnp.bfloat16)
    term_x = lax.all_to_all(derived, "grid", split_axis=1, concat_axis=2, tiled=True)
    return -0.5 * (term_x.astype(jnp.float32) + term_y + term_z) + potential[None] * field.astype(
        jnp.float32
    )


def ritz(correlation, hamil):
    scale = jnp.max(jnp.sum(jnp.abs(correlation), axis=1))
    current = correlation / scale
    identity = jnp.eye(correlation.shape[0], dtype=jnp.float32)
    inverse_root = identity
    for turn_index in range(NS_ITERS):
        turn = 1.5 * identity - 0.5 * jnp.dot(
            inverse_root, current, precision=lax.Precision.HIGHEST
        )
        current = jnp.dot(current, turn, precision=lax.Precision.HIGHEST)
        inverse_root = jnp.dot(turn, inverse_root, precision=lax.Precision.HIGHEST)
    projected = (
        jnp.dot(
            jnp.dot(inverse_root.T, hamil, precision=lax.Precision.HIGHEST),
            inverse_root,
            precision=lax.Precision.HIGHEST,
        )
        / scale
    )
    return (inverse_root.astype(jnp.bfloat16), projected)


def inner_rows(left, right):
    return lax.dot_general(
        left, right, (((1,), (1,)), ((), ())), preferred_element_type=jnp.float32
    )


def per_device(orbitals, potential):
    own = orbitals.shape[0]
    k_x = second_derivative(orbitals.shape[1] * lax.axis_size("grid"))
    k_y = second_derivative(orbitals.shape[2])
    k_z = second_derivative(orbitals.shape[3])
    start_f = orbitals.astype(jnp.float32)
    first = (
        (apply_ham(orbitals, potential, k_x, k_y, k_z) - CENTER * start_f) / HALF_WIDTH
    ).astype(jnp.bfloat16)
    first_f = first.astype(jnp.float32)
    filtered = (
        2.0 * (apply_ham(first, potential, k_x, k_y, k_z) - CENTER * first_f) / HALF_WIDTH - start_f
    ).astype(jnp.bfloat16)
    applied = apply_ham(filtered, potential, k_x, k_y, k_z).astype(jnp.bfloat16)
    gathered = lax.all_gather(filtered, "band", axis=0, tiled=True)
    total = gathered.shape[0]
    flat = gathered.reshape(total, -1)
    s_rows = inner_rows(filtered.reshape(own, -1), flat)
    h_rows = inner_rows(applied.reshape(own, -1), flat)
    s_rows, h_rows = lax.psum((s_rows, h_rows), "grid")
    correlation, hamil = (
        lax.all_gather(s_rows, "band", axis=0, tiled=True),
        lax.all_gather(h_rows, "band", axis=0, tiled=True),
    )
    coeff, projected = ritz(correlation, hamil)
    columns = lax.dynamic_slice_in_dim(coeff, lax.axis_index("band") * own, own, 1)
    mine = lax.dot_general(
        columns, flat, (((0,), (0,)), ((), ())), preferred_element_type=jnp.float32
    )
    rotated = mine.astype(jnp.bfloat16).reshape(filtered.shape)
    return (rotated, projected)


def solution(mesh):
    in_specs = (P("band", "grid", None, None), P("grid", None, None))
    out_specs = (P("band", "grid", None, None), P())
    return jax.shard_map(
        per_device, mesh=mesh, in_specs=in_specs, out_specs=out_specs, check_vma=False
    )
```

profile of v0, /device:TPU:0, one launch (start us, length us, event | category | flops | bytes accessed | tf_op | source)
XLA Modules:
  0.0 1303.1 jit_solution(14852924869631262509)
XLA Ops:
  7.2 11.6 copy.65
  26.9 91.7 %all-to-all-done = bf16[2,32,256,256]{3,1,0,2:T(8,128)(2,1)} async-done(((bf16[2,32,256,256]{3,1,0,2:T(8,128)(2,1)}), bf16[2,32,256,256]{3,1,0,2:T(8,128)(2,1)}, u32[]{:S(2)}, u32[]{:S(2)}) %all-to-all-start) | async-done | bytes 8388640 | tf_op jit(solution)/shard_map/all_to_all | solution.py:33
  135.8 11.5 copy.68
  152.5 11.5 convolution_bitcast_fusion
  164.0 17.5 %copy.71 = f32[16384,256]{1,0:T(8,128)} copy(f32[16384,256]{0,1:T(8,128)} %convolution_bitcast_fusion) | data formatting | bytes 33554432 | tf_op jit(solution)/shard_map/dot_general | solution.py:27
  181.5 65.1 %all-to-all-done.1 = bf16[2,256,32,256]{3,2,0,1:T(8,128)(2,1)} async-done(((bf16[2,256,32,256]{3,2,0,1:T(8,128)(2,1)}), bf16[2,256,32,256]{3,2,0,1:T(8,128)(2,1)}, u32[]{:S(2)}, u32[]{:S(2)}) %all-to-all-start.1) | async-done | bytes 8388640 | tf_op jit(solution)/shard_map/all_to_all | solution.py:37
  257.9 23.2 %fusion.10 = bf16[2,32,256,256]{3,2,1,0:T(8,128)(2,1)} fusion(bf16[2,32,256,256]{3,2,1,0:T(8,128)(2,1)} %param.2, f32[2,32,256,256]{3,2,1,0:T(8,128)} %bitcast.160, f32[2,8,32,32,256]{4,3,1,2,0:T(8,128)} %copy.69, f32[32,256,256]{2,1,0:T(8,128)} %param.3, bf16[256,256]{1,0:T(8,128)(2,1)S(1)} %fusion.22), kind=kOutput, calls=%fused_computation.17 | convolution fusion | flops 2189426688 | bytes 58851328 | tf_op jit(solution)/shard_map/oxjz,jy->oxyz/dot_general | solution.py:30
  292.5 100.1 %all_to_all.81 = bf16[2,32,256,256]{3,1,0,2:T(8,128)(2,1)} all-to-all(bf16[2,32,256,256]{3,1,0,2:T(8,128)(2,1)} %copy.72), channel_id=1, replica_groups=mesh['band'=4,'grid'=8] {'grid'}, dimensions={2} | all-to-all | bytes 16777216 | tf_op jit(solution)/shard_map/all_to_all | solution.py:33
  409.6 11.4 copy.75
  426.2 11.5 fusion.55
  437.6 82.3 %all-to-all-done.3 = bf16[2,256,32,256]{3,2,0,1:T(8,128)(2,1)} async-done(((bf16[2,256,32,256]{3,2,0,1:T(8,128)(2,1)}), bf16[2,256,32,256]{3,2,0,1:T(8,128)(2,1)}, u32[]{:S(2)}, u32[]{:S(2)}) %all-to-all-start.3) | async-done | bytes 8388640 | tf_op jit(solution)/shard_map/all_to_all | solution.py:37
  531.3 26.1 %fusion.11 = bf16[2,32,256,256]{3,2,1,0:T(8,128)(2,1)} fusion(bf16[2,32,256,256]{3,2,1,0:T(8,128)(2,1)} %param.2, bf16[2,32,256,256]{3,2,1,0:T(8,128)(2,1)} %fusion.10, f32[2,8,32,32,256]{4,3,1,2,0:T(8,128)} %copy.76, f32[256,2,32,256]{3,0,2,1:T(8,128)} %fusion.55, f32[32,256,256]{2,1,0:T(8,128)} %param.3, bf16[256,256]{1,0:T(8,128)(2,1)S(1)} %fusion.22), kind=kOutput, calls=%fused_computation.18 | convolution fusion | flops 2197815296 | bytes 67239936 | tf_op jit(solution)/shard_map/dot_general | solution.py:27
  557.4 13.7 %copy.81 = bf16[2,32,256,256]{3,1,0,2:T(8,128)(2,1)} copy(bf16[2,32,256,256]{3,2,1,0:T(8,128)(2,1)} %fusion.11) | data formatting | bytes 16777216 | tf_op jit(solution)/shard_map/convert_element_type | solution.py:83
  571.1 100.2 %all_to_all.82 = bf16[2,32,256,256]{3,1,0,2:T(8,128)(2,1)} all-to-all(bf16[2,32,256,256]{3,1,0,2:T(8,128)(2,1)} %copy.81), channel_id=1, replica_groups=mesh['band'=4,'grid'=8] {'grid'}, dimensions={2} | all-to-all | bytes 16777216 | tf_op jit(solution)/shard_map/all_to_all | solution.py:33
  688.6 11.6 copy.84
  705.2 11.5 fusion.50
  716.6 82.6 %all-to-all-done.5 = bf16[2,256,32,256]{3,2,0,1:T(8,128)(2,1)} async-done(((bf16[2,256,32,256]{3,2,0,1:T(8,128)(2,1)}), bf16[2,256,32,256]{3,2,0,1:T(8,128)(2,1)}, u32[]{:S(2)}, u32[]{:S(2)}) %all-to-all-start.5) | async-done | bytes 8388640 | tf_op jit(solution)/shard_map/all_to_all | solution.py:37
  810.5 23.3 %fusion.15 = bf16[2,32,256,256]{3,2,1,0:T(8,128)(2,1)} fusion(f32[2,8,32,32,256]{4,3,1,2,0:T(8,128)} %copy.85, f32[256,2,32,256]{3,0,2,1:T(8,128)} %fusion.50, bf16[2,32,256,256]{3,2,1,0:T(8,128)(2,1)} %fusion.11, f32[32,256,256]{2,1,0:T(8,128)} %param.3, bf16[256,256]{1,0:T(8,128)(2,1)S(1)} %fusion.22), kind=kOutput, calls=%fused_computation.23 | convolution fusion | flops 2176843776 | bytes 58851328 | tf_op jit(solution)/shard_map/dot_general | solution.py:27
  833.8 285.2 %all-gather.4.cloned.1.call-done = bf16[8,32,256,256]{3,2,1,0:T(8,128)(2,1)} async-done(((bf16[2,32,256,256]{3,2,1,0:T(8,128)(2,1)}), bf16[8,32,256,256]{3,2,1,0:T(8,128)(2,1)}) %all-gather.4.cloned.1.call-update) | async-done | bytes 33554448 | tf_op jit(solution)/shard_map/all_gather | solution.py:85
  1119.0 49.8 %fusion.29 = f32[2,8]{1,0:T(2,128)S(1)} fusion(bf16[8,32,256,256]{3,2,1,0:T(8,128)(2,1)} %all-gather.4.cloned.1.call-done, bf16[2,32,256,256]{3,2,1,0:T(8,128)(2,1)} %fusion.11), kind=kOutput, calls=%fused_computation.50 | convolution fusion | flops 67108864 | bytes 41943104 | tf_op jit(solution)/shard_map/dot_general | solution.py:66
  1168.8 34.6 %fusion.34 = f32[2,8]{1,0:T(2,128)S(1)} fusion(bf16[8,32,256,256]{3,2,1,0:T(8,128)(2,1)} %all-gather.4.cloned.1.call-done, bf16[2,32,256,256]{3,2,1,0:T(8,128)(2,1)S(1)} %copy-done), kind=kOutput, calls=%fused_computation.51 | convolution fusion | flops 67108864 | bytes 41943104 | tf_op jit(solution)/shard_map/dot_general | solution.py:66
  1203.4 13.8 %all-reduce = (f32[2,8]{1,0:T(2,128)S(1)}, f32[2,8]{1,0:T(2,128)S(1)}) all-reduce(f32[2,8]{1,0:T(2,128)S(1)} %fusion.29, f32[2,8]{1,0:T(2,128)S(1)} %fusion.34), channel_id=1, replica_groups=mesh['band'=4,'grid'=8] {'grid'}, use_global_device_ids=true, to_apply=%region_0.1 | all-reduce | flops 32 | bytes 256 | tf_op jit(solution)/shard_map/psum | solution.py:90
  1239.5 31.1 %copy.105 = bf16[1,8,8192,256]{3,1,2,0:T(8,128)(2,1)} copy(bf16[1,8,8192,256]{3,2,1,0:T(8,128)(2,1)} %bitcast.162) | data formatting | bytes 67108864
  1270.6 17.5 %convolution_convert_fusion = bf16[2,2097152]{1,0:T(2,128)(2,1)} fusion(bf16[8,2097152]{1,0:T(8,128)(2,1)} %bitcast.158, bf16[8,8]{0,1:T(8,128)(2,1)S(1)} %get-tuple-element.4, s32[]{:T(128)S(6)} %select_n.21), kind=kOutput, calls=%fused_computation | convolution fusion | flops 71303168 | bytes 41943556 | tf_op jit(solution)/shard_map/dot_general | solution.py:97
  (46 shorter events, 150.5 us)
Async XLA Ops:
  18.7 99.9 %all-to-all-start = ((bf16[2,32,256,256]{3,1,0,2:T(8,128)(2,1)}), bf16[2,32,256,256]{3,1,0,2:T(8,128)(2,1)}, u32[]{:S(2)}, u32[]{:S(2)}) async-start(bf16[2,32,256,256]{3,1,0,2:T(8,128)(2,1)} %copy.65), calls=%async_computation | async-start | bytes 16777216 | tf_op jit(solution)/shard_map/all_to_all | solution.py:33
  147.4 99.2 %all-to-all-start.1 = ((bf16[2,256,32,256]{3,2,0,1:T(8,128)(2,1)}), bf16[2,256,32,256]{3,2,0,1:T(8,128)(2,1)}, u32[]{:S(2)}, u32[]{:S(2)}) async-start(bf16[2,256,32,256]{3,2,0,1:T(8,128)(2,1)} %copy.68), calls=%async_computation.1 | async-start | bytes 16777216 | tf_op jit(solution)/shard_map/all_to_all | solution.py:37
  421.0 99.0 %all-to-all-start.3 = ((bf16[2,256,32,256]{3,2,0,1:T(8,128)(2,1)}), bf16[2,256,32,256]{3,2,0,1:T(8,128)(2,1)}, u32[]{:S(2)}, u32[]{:S(2)}) async-start(bf16[2,256,32,256]{3,2,0,1:T(8,128)(2,1)} %copy.75), calls=%async_computation.3 | async-start | bytes 16777216 | tf_op jit(solution)/shard_map/all_to_all | solution.py:37
  425.9 693.1 %all-gather.4.cloned.1.call-start = ((), (), s32[]{:S(2)}) async-start(), calls=%async_computation.6 | async-start | bytes 41943040 | tf_op jit(solution)/shard_map/all_gather | solution.py:85
  700.2 99.0 %all-to-all-start.5 = ((bf16[2,256,32,256]{3,2,0,1:T(8,128)(2,1)}), bf16[2,256,32,256]{3,2,0,1:T(8,128)(2,1)}, u32[]{:S(2)}, u32[]{:S(2)}) async-start(bf16[2,256,32,256]{3,2,0,1:T(8,128)(2,1)} %copy.84), calls=%async_computation.5 | async-start | bytes 16777216 | tf_op jit(solution)/shard_map/all_to_all | solution.py:37
  1119.0 49.8 %copy-start = (bf16[2,32,256,256]{3,2,1,0:T(8,128)(2,1)S(1)}, bf16[2,32,256,256]{3,2,1,0:T(8,128)(2,1)}, u32[]{:S(2)}) copy-start(bf16[2,32,256,256]{3,2,1,0:T(8,128)(2,1)} %fusion.15) | copy-start | bytes 25165828
Sparse Core Ops, SparseCore 0:
  557.5 561.5 all-gather.3
where the time goes:
time: 1310 us; the launch traced here: 1300 us
  waiting for transfers between devices  607 us (46%)
  matrix products  242 us (18%)
  blocking collectives  231 us (18%)
  local copies, waits for them, and re-layouts  186 us (14%)
  starting transfers between devices  20.7 us (2%)
  between operations  14.3 us (1%)
    all_gather x1, waiting for transfers between devices, per_device(): gathered = lax.all_gather(filtered, 'band', axis=0, tiled=True)  285 us
    all_to_all x3, waiting for transfers between devices, apply_ham(): lax.all_to_all(derived, 'grid', split_axis=1, concat_axis=2, tiled=True)  230 us
    all_to_all x2, blocking collectives, apply_ham(): lax.all_to_all(field, 'grid', split_axis=2, concat_axis=1, tiled=True)  200 us
    all_to_all x1, waiting for transfers between devices, apply_ham(): lax.all_to_all(field, 'grid', split_axis=2, concat_axis=1, tiled=True)  91.7 us
    dot_general x2, matrix products, inner_rows(): lax.dot_general(left, right, (((1,), (1,)), ((), ())), preferred_element_...  84.3 us
    dot_general x3, matrix products, apply_ham(): jnp.dot(field.reshape(-1, depth), k_z, preferred_element_type=jnp.float32)  60.8 us
    unnamed x5, local copies, waits for them, and re-layouts  50.5 us
    dot_general x3, matrix products, apply_ham(): jnp.einsum('oxjz,jy->oxyz', field, k_y, preferred_element_type=jnp.float32)  46.2 us
  transfers between devices with their start and end apart: 5, of which 5 were waited for; matrix products, arithmetic and copies ran while one was open for 10% of the time, Pallas kernels for 0%

commit v1 on v0

--- a/solution.py
+++ b/solution.py
@@ -82,7 +82,12 @@
         2.0 * (apply_ham(first, potential, k_x, k_y, k_z) - CENTER * first_f) / HALF_WIDTH - start_f
     ).astype(jnp.bfloat16)
     applied = apply_ham(filtered, potential, k_x, k_y, k_z).astype(jnp.bfloat16)
-    gathered = lax.all_gather(filtered, "band", axis=0, tiled=True)
+    ring = [filtered]
+    for hop in range(3):
+        ring.append(lax.ppermute(ring[-1], "band", [(dev, (dev + 1) % 4) for dev in range(4)]))
+    gathered = jnp.roll(
+        jnp.concatenate(ring[::-1], axis=0), (lax.axis_index("band") + 1) * ring[0].shape[0], axis=0
+    )
     total = gathered.shape[0]
     flat = gathered.reshape(total, -1)
     s_rows = inner_rows(filtered.reshape(own, -1), flat)

time: 1310 us -> 1380 us (1.053)
  blocking collectives: 231 us -> 136 us
  local copies, waits for them, and re-layouts: 186 us -> 268 us
  waiting for transfers between devices: 607 us -> 684 us
  matrix products: 242 us -> 257 us
    ppermute x0 -> x3, waiting for transfers between devices: none -> 444 us  [per_device(): lax.ppermute(ring[-1], 'band', [(dev, (dev + 1) % 4) for dev in range(4)])]
    all_gather x1 -> x0, waiting for transfers between devices: 285 us -> none  [per_device(): gathered = lax.all_gather(filtered, 'band', axis=0, tiled=True)]
    all_to_all x2 -> x1, blocking collectives: 200 us -> 99.9 us  [apply_ham(): lax.all_to_all(field, 'grid', split_axis=2, concat_axis=1, tiled=True)]
    all_to_all x3, waiting for transfers between devices: 230 us -> 148 us  [apply_ham(): lax.all_to_all(derived, 'grid', split_axis=1, concat_axis=2, tiled=True)]
    unnamed x5 -> x10, local copies, waits for them, and re-layouts: 50.5 us -> 104 us
    dynamic_slice x0 -> x1, local copies, waits for them, and re-layouts: none -> 23 us  [per_device(): jnp.roll(jnp.concatenate(ring[::-1], axis=0), (lax.axis_index('band') + 1...]
    dot_general x2, matrix products: 84.3 us -> 99.6 us  [inner_rows(): lax.dot_general(left, right, (((1,), (1,)), ((), ())), preferred_element_...]
    all_to_all x1 -> x2, waiting for transfers between devices: 91.7 us -> 91.7 us  [apply_ham(): lax.all_to_all(field, 'grid', split_axis=2, concat_axis=1, tiled=True)]
  transfers between devices with their start and end apart: 5 -> 8, of which waited for: 5 -> 6; matrix products, arithmetic and copies ran while one was open for 10% -> 9% of each run, Pallas kernels for 0% -> 0%
where the time goes in v1:
time: 1380 us
  waiting for transfers between devices  684 us (50%)
  local copies, waits for them, and re-layouts  268 us (19%)
  matrix products  257 us (19%)
  blocking collectives  136 us (10%)
  starting transfers between devices  29 us (2%)
    ppermute x3, waiting for transfers between devices, per_device(): lax.ppermute(ring[-1], 'band', [(dev, (dev + 1) % 4) for dev in range(4)])  444 us
    all_to_all x3, waiting for transfers between devices, apply_ham(): lax.all_to_all(derived, 'grid', split_axis=1, concat_axis=2, tiled=True)  148 us
    unnamed x10, local copies, waits for them, and re-layouts  104 us
    all_to_all x1, blocking collectives, apply_ham(): lax.all_to_all(field, 'grid', split_axis=2, concat_axis=1, tiled=True)  99.9 us
    dot_general x2, matrix products, inner_rows(): lax.dot_general(left, right, (((1,), (1,)), ((), ())), preferred_element_...  99.6 us
    all_to_all x2, waiting for transfers between devices, apply_ham(): lax.all_to_all(field, 'grid', split_axis=2, concat_axis=1, tiled=True)  91.7 us
    dot_general x3, matrix products, apply_ham(): jnp.dot(field.reshape(-1, depth), k_z, preferred_element_type=jnp.float32)  60.6 us
    dot_general x3, matrix products, apply_ham(): jnp.einsum('oxjz,jy->oxyz', field, k_y, preferred_element_type=jnp.float32)  46.2 us
  transfers between devices with their start and end apart: 8, of which 6 were waited for; matrix products, arithmetic and copies ran while one was open for 9% of the time, Pallas kernels for 0%

profile of v1, /device:TPU:0, one launch (start us, length us, event | category | flops | bytes accessed | tf_op | source)
XLA Modules:
  0.0 1376.2 jit_solution(7244123992208639853)
XLA Ops:
  0.6 11.6 copy.65
  20.5 91.7 %all-to-all-done = bf16[2,32,256,256]{3,1,0,2:T(8,128)(2,1)} async-done(((bf16[2,32,256,256]{3,1,0,2:T(8,128)(2,1)}), bf16[2,32,256,256]{3,1,0,2:T(8,128)(2,1)}, u32[]{:S(2)}, u32[]{:S(2)}) %all-to-all-start) | async-done | bytes 8388640 | tf_op jit(solution)/shard_map/all_to_all | solution.py:33
  129.4 11.5 copy.68
  146.4 11.5 convolution_bitcast_fusion
  158.0 17.4 %copy.71 = f32[16384,256]{1,0:T(8,128)} copy(f32[16384,256]{0,1:T(8,128)} %convolution_bitcast_fusion) | data formatting | bytes 33554432 | tf_op jit(solution)/shard_map/dot_general | solution.py:27
  175.4 65.1 %all-to-all-done.1 = bf16[2,256,32,256]{3,2,0,1:T(8,128)(2,1)} async-done(((bf16[2,256,32,256]{3,2,0,1:T(8,128)(2,1)}), bf16[2,256,32,256]{3,2,0,1:T(8,128)(2,1)}, u32[]{:S(2)}, u32[]{:S(2)}) %all-to-all-start.1) | async-done | bytes 8388640 | tf_op jit(solution)/shard_map/all_to_all | solution.py:37
  251.8 23.3 %fusion.10 = bf16[2,32,256,256]{3,2,1,0:T(8,128)(2,1)} fusion(bf16[2,32,256,256]{3,2,1,0:T(8,128)(2,1)} %param.2, f32[2,32,256,256]{3,2,1,0:T(8,128)} %bitcast.161, f32[2,8,32,32,256]{4,3,1,2,0:T(8,128)} %copy.69, f32[32,256,256]{2,1,0:T(8,128)} %param.3, bf16[256,256]{1,0:T(8,128)(2,1)S(1)} %fusion.22), kind=kOutput, calls=%fused_computation.17 | convolution fusion | flops 2189426688 | bytes 58851328 | tf_op jit(solution)/shard_map/oxjz,jy->oxyz/dot_general | solution.py:30
  286.4 99.9 %all_to_all.81 = bf16[2,32,256,256]{3,1,0,2:T(8,128)(2,1)} all-to-all(bf16[2,32,256,256]{3,1,0,2:T(8,128)(2,1)} %copy.72), channel_id=1, replica_groups=mesh['band'=4,'grid'=8] {'grid'}, dimensions={2} | all-to-all | bytes 16777216 | tf_op jit(solution)/shard_map/all_to_all | solution.py:33
  419.9 11.5 fusion.55
  431.4 82.6 %all-to-all-done.3 = bf16[2,256,32,256]{3,2,0,1:T(8,128)(2,1)} async-done(((bf16[2,256,32,256]{3,2,0,1:T(8,128)(2,1)}), bf16[2,256,32,256]{3,2,0,1:T(8,128)(2,1)}, u32[]{:S(2)}, u32[]{:S(2)}) %all-to-all-start.3) | async-done | bytes 8388640 | tf_op jit(solution)/shard_map/all_to_all | solution.py:37
  525.3 26.1 %fusion.11 = bf16[2,32,256,256]{3,2,1,0:T(8,128)(2,1)} fusion(bf16[2,32,256,256]{3,2,1,0:T(8,128)(2,1)} %param.2, bf16[2,32,256,256]{3,2,1,0:T(8,128)(2,1)} %fusion.10, f32[2,8,32,32,256]{4,3,1,2,0:T(8,128)} %copy.76, f32[256,2,32,256]{3,0,2,1:T(8,128)} %fusion.55, f32[32,256,256]{2,1,0:T(8,128)} %param.3, bf16[256,256]{1,0:T(8,128)(2,1)S(1)} %fusion.22), kind=kOutput, calls=%fused_computation.18 | convolution fusion | flops 2197815296 | bytes 67239936 | tf_op jit(solution)/shard_map/dot_general | solution.py:27
  553.6 11.6 copy.81
  570.2 163.3 %collective-permute-done = bf16[2,32,256,256]{3,2,1,0:T(8,128)(2,1)} collective-permute-done((bf16[2,32,256,256]{3,2,1,0:T(8,128)(2,1)}, bf16[2,32,256,256]{3,2,1,0:T(8,128)(2,1)}, u32[]{:S(2)}, u32[]{:S(2)}) %collective-permute-start) | collective-permute-done | bytes 8388640 | tf_op jit(solution)/shard_map/ppermute | solution.py:87
  751.2 11.5 copy.84
  767.7 147.0 %collective-permute-done.1 = bf16[2,32,256,256]{3,2,1,0:T(8,128)(2,1)} collective-permute-done((bf16[2,32,256,256]{3,2,1,0:T(8,128)(2,1)}, bf16[2,32,256,256]{3,2,1,0:T(8,128)(2,1)}, u32[]{:S(2)}, u32[]{:S(2)}) %collective-permute-start.1) | collective-permute-done | bytes 8388640 | tf_op jit(solution)/shard_map/ppermute | solution.py:87
  914.9 11.5 fusion.50
  937.7 23.0 %fusion.15 = bf16[2,32,256,256]{3,2,1,0:T(8,128)(2,1)} fusion(f32[2,8,32,32,256]{4,3,1,2,0:T(8,128)} %copy.85, f32[256,2,32,256]{3,0,2,1:T(8,128)} %fusion.50, bf16[2,32,256,256]{3,2,1,0:T(8,128)(2,1)} %fusion.11, f32[32,256,256]{2,1,0:T(8,128)} %param.3, bf16[256,256]{1,0:T(8,128)(2,1)S(1)} %fusion.22), kind=kOutput, calls=%fused_computation.23 | convolution fusion | flops 2176843776 | bytes 58851328 | tf_op jit(solution)/shard_map/dot_general | solution.py:27
  960.7 134.1 %collective-permute-done.2 = bf16[2,32,256,256]{3,2,1,0:T(8,128)(2,1)} collective-permute-done((bf16[2,32,256,256]{3,2,1,0:T(8,128)(2,1)}, bf16[2,32,256,256]{3,2,1,0:T(8,128)(2,1)}, u32[]{:S(2)}, u32[]{:S(2)}) %collective-permute-start.2) | collective-permute-done | bytes 8388640 | tf_op jit(solution)/shard_map/ppermute | solution.py:87
  1155.6 23.0 %constant_dynamic-slice_fusion = bf16[8,32,256,256]{3,2,1,0:T(8,128)(2,1)} fusion(bf16[16,32,256,256]{3,2,1,0:T(8,128)(2,1)} %constant_dynamic-update-slice_fusion, s32[]{:T(128)S(6)} %select_n.34), kind=kLoop, calls=%fused_computation.99 | loop fusion | bytes 67108864 | tf_op jit(solution)/shard_map/jit(_roll_dynamic)/dynamic_slice | solution.py:88
  1178.6 49.7 %fusion.29 = f32[2,8]{1,0:T(2,128)S(1)} fusion(bf16[8,32,256,256]{3,2,1,0:T(8,128)(2,1)} %constant_dynamic-slice_fusion, bf16[2,32,256,256]{3,2,1,0:T(8,128)(2,1)} %fusion.11), kind=kOutput, calls=%fused_computation.50 | convolution fusion | flops 67108864 | bytes 41943104 | tf_op jit(solution)/shard_map/dot_general | solution.py:66
  1228.3 49.9 %fusion.34 = f32[2,8]{1,0:T(2,128)S(1)} fusion(bf16[8,32,256,256]{3,2,1,0:T(8,128)(2,1)} %constant_dynamic-slice_fusion, bf16[2,32,256,256]{3,2,1,0:T(8,128)(2,1)} %fusion.15), kind=kOutput, calls=%fused_computation.51 | convolution fusion | flops 67108864 | bytes 41943104 | tf_op jit(solution)/shard_map/dot_general | solution.py:66
  1278.1 18.8 %all-reduce = (f32[2,8]{1,0:T(2,128)S(1)}, f32[2,8]{1,0:T(2,128)S(1)}) all-reduce(f32[2,8]{1,0:T(2,128)S(1)} %fusion.29, f32[2,8]{1,0:T(2,128)S(1)} %fusion.34), channel_id=1, replica_groups=mesh['band'=4,'grid'=8] {'grid'}, use_global_device_ids=true, to_apply=%region_0.1 | all-reduce | flops 32 | bytes 256 | tf_op jit(solution)/shard_map/psum | solution.py:95
  1319.4 31.2 %copy.105 = bf16[1,8,8192,256]{3,1,2,0:T(8,128)(2,1)} copy(bf16[1,8,8192,256]{3,2,1,0:T(8,128)(2,1)} %bitcast.159) | data formatting | bytes 67108864
  1350.6 17.5 %convolution_convert_fusion = bf16[2,2097152]{1,0:T(2,128)(2,1)} fusion(bf16[8,2097152]{1,0:T(8,128)(2,1)} %bitcast.158, bf16[8,8]{0,1:T(8,128)(2,1)S(1)} %get-tuple-element.4, s32[]{:T(128)S(6)} %select_n.35), kind=kOutput, calls=%fused_computation | convolution fusion | flops 71303168 | bytes 41943556 | tf_op jit(solution)/shard_map/dot_general | solution.py:102
  (57 shorter events, 230.9 us)
Async XLA Ops:
  12.2 100.0 %all-to-all-start = ((bf16[2,32,256,256]{3,1,0,2:T(8,128)(2,1)}), bf16[2,32,256,256]{3,1,0,2:T(8,128)(2,1)}, u32[]{:S(2)}, u32[]{:S(2)}) async-start(bf16[2,32,256,256]{3,1,0,2:T(8,128)(2,1)} %copy.65), calls=%async_computation | async-start | bytes 16777216 | tf_op jit(solution)/shard_map/all_to_all | solution.py:33
  141.0 99.5 %all-to-all-start.1 = ((bf16[2,256,32,256]{3,2,0,1:T(8,128)(2,1)}), bf16[2,256,32,256]{3,2,0,1:T(8,128)(2,1)}, u32[]{:S(2)}, u32[]{:S(2)}) async-start(bf16[2,256,32,256]{3,2,0,1:T(8,128)(2,1)} %copy.68), calls=%async_computation.1 | async-start | bytes 16777216 | tf_op jit(solution)/shard_map/all_to_all | solution.py:37
  414.7 99.2 %all-to-all-start.3 = ((bf16[2,256,32,256]{3,2,0,1:T(8,128)(2,1)}), bf16[2,256,32,256]{3,2,0,1:T(8,128)(2,1)}, u32[]{:S(2)}, u32[]{:S(2)}) async-start(bf16[2,256,32,256]{3,2,0,1:T(8,128)(2,1)} %copy.75), calls=%async_computation.3 | async-start | bytes 16777216 | tf_op jit(solution)/shard_map/all_to_all | solution.py:37
  551.3 182.2 %collective-permute-start = (bf16[2,32,256,256]{3,2,1,0:T(8,128)(2,1)}, bf16[2,32,256,256]{3,2,1,0:T(8,128)(2,1)}, u32[]{:S(2)}, u32[]{:S(2)}) collective-permute-start(bf16[2,32,256,256]{3,2,1,0:T(8,128)(2,1)} %fusion.11), channel_id=1, source_target_pairs={{0,8},{8,16},{16,24},{24,0},{1,9},{9,17},{17,25},{25,1},{2,10},{10... | collective-permute-start | bytes 25165832 | tf_op jit(solution)/shard_map/ppermute | solution.py:87
  565.2 168.7 %all-to-all-start.4 = ((bf16[2,32,256,256]{3,1,0,2:T(8,128)(2,1)}), bf16[2,32,256,256]{3,1,0,2:T(8,128)(2,1)}, u32[]{:S(2)}, u32[]{:S(2)}) async-start(bf16[2,32,256,256]{3,1,0,2:T(8,128)(2,1)} %copy.81), calls=%async_computation.4 | async-start | bytes 16777216 | tf_op jit(solution)/shard_map/all_to_all | solution.py:33
  733.5 181.2 %collective-permute-start.1 = (bf16[2,32,256,256]{3,2,1,0:T(8,128)(2,1)}, bf16[2,32,256,256]{3,2,1,0:T(8,128)(2,1)}, u32[]{:S(2)}, u32[]{:S(2)}) collective-permute-start(bf16[2,32,256,256]{3,2,1,0:T(8,128)(2,1)} %collective-permute-done), channel_id=1, source_target_pairs={{0,8},{8,16},{16,24},{24,0},{1,9},{9,17},{17,25},{25,1},{2,10},{10... | collective-permute-start | bytes 25165832 | tf_op jit(solution)/shard_map/ppermute | solution.py:87
  762.7 163.7 %all-to-all-start.5 = ((bf16[2,256,32,256]{3,2,0,1:T(8,128)(2,1)}), bf16[2,256,32,256]{3,2,0,1:T(8,128)(2,1)}, u32[]{:S(2)}, u32[]{:S(2)}) async-start(bf16[2,256,32,256]{3,2,0,1:T(8,128)(2,1)} %copy.84), calls=%async_computation.5 | async-start | bytes 16777216 | tf_op jit(solution)/shard_map/all_to_all | solution.py:37
  914.8 180.1 %collective-permute-start.2 = (bf16[2,32,256,256]{3,2,1,0:T(8,128)(2,1)}, bf16[2,32,256,256]{3,2,1,0:T(8,128)(2,1)}, u32[]{:S(2)}, u32[]{:S(2)}) collective-permute-start(bf16[2,32,256,256]{3,2,1,0:T(8,128)(2,1)} %collective-permute-done.1), channel_id=1, source_target_pairs={{0,8},{8,16},{16,24},{24,0},{1,9},{9,17},{17,25},{25,1},{2,10},{10... | collective-permute-start | bytes 25165832 | tf_op jit(solution)/shard_map/ppermute | solution.py:87
